TPU v7x, 512 devices: a whole 4x8x8 slice. The times are simulated.
512 devices in a mesh: dp: 4 (over x), expert: 64 (over z, y), tensor: 2 (over core).
Axes of the slice: x: 4, y: 8, z: 8, core: 2. Of those that a mesh axis runs over, the one named last changes fastest.
Arguments:
- out_grad: bfloat16 [32768, 3584], P(('dp', 'expert'), 'tensor'), may hold values from -6 to 6
- routing: int32 [32768, 8], P(('dp', 'expert')), may hold values from 0 to 255, all different within a row; in each aligned block of 128 rows (0 to 127, 128 to 255, ...) at most 8 rows name the same one
- route_probs: float32 [32768, 8], P(('dp', 'expert')), may hold values from 0.05 to 1
- w_down: bfloat16 [64, 3584, 1024], P('expert', 'dp', 'tensor'), may hold values from -0.1875 to 0.1875
- saved_gate: bfloat16 [131072, 1024], P(('dp', 'expert'), 'tensor'), may hold values from -8 to 8
- saved_up: bfloat16 [131072, 1024], P(('dp', 'expert'), 'tensor'), may hold values from -6 to 6
Outputs:
- weight_grad: bfloat16 [64, 3584, 1024], P('expert', 'dp', 'tensor')
- grad_gate: bfloat16 [131072, 1024], P(('dp', 'expert'), 'tensor')
- grad_up: bfloat16 [131072, 1024], P(('dp', 'expert'), 'tensor')
- grad_amax: float32 [4, 64], P('dp', 'expert')
Inputs may be any that keep to these rules, and one draw needn't show every extreme that they name: `routing`: each row names 8 different experts; in the rows of one device no expert is named more than 8 times.
All inputs are finite; a program needn't handle non-finite values. Where the computation divides by a largest or mean magnitude, that divisor is 1e-20 or more.
Results may differ from a plain program's by a relative error of at most 0.009.
Values may be sent and summed in bfloat16 or wider, within the bound.
A program may use at most 64 MiB of HBM per device.

v0:
```python
import jax
import jax.numpy as jnp
from jax import lax
from jax.sharding import PartitionSpec as P

epsilon = 1e-06


def slot_tables(routing, route_probs, owners, capacity):
    tok_count = routing.shape[0]
    matches = routing[:, :, None] == jnp.arange(owners, dtype=jnp.int32)[None, None, :]
    is_routed = jnp.any(matches, axis=1).astype(jnp.int32)
    scaling = jnp.sum(jnp.where(matches, route_probs[:, :, None], 0.0), axis=1)
    slot_rank = jnp.cumsum(is_routed, axis=0) - is_routed
    picked = (is_routed[:, :, None] == 1) & (
        slot_rank[:, :, None] == jnp.arange(capacity, dtype=jnp.int32)[None, None, :]
    )
    token_ids = jnp.arange(tok_count, dtype=jnp.int32)[:, None, None]
    slot_token = jnp.sum(jnp.where(picked, token_ids, 0), axis=0)
    slot_scale = jnp.sum(jnp.where(picked, scaling[:, :, None], 0.0), axis=0)
    return (slot_token, slot_scale)


def body(out_grad, routing, route_probs, w_down, saved_gate, saved_up):
    owners = lax.axis_size("expert")
    slot_count = saved_gate.shape[0]
    capacity = slot_count // owners
    slot_token, slot_scale = slot_tables(routing, route_probs, owners, capacity)
    features = lax.all_gather(out_grad, "tensor", axis=1, tiled=True)
    picked_rows = jnp.take(features, slot_token, axis=0)
    arrived = lax.all_to_all(
        (picked_rows.astype(jnp.float32) * slot_scale[:, :, None]).astype(jnp.bfloat16),
        "expert",
        split_axis=0,
        concat_axis=0,
        tiled=True,
    )
    slot_rows = arrived.reshape(slot_count, features.shape[1])
    columns = slot_rows
    grad_hidden = jnp.dot(
        columns,
        lax.all_gather(w_down, "dp", axis=1, tiled=True)[0],
        preferred_element_type=jnp.float32,
    )
    gate_pre = saved_gate.astype(jnp.float32)
    up_pre = saved_up.astype(jnp.float32)
    sigmoid_gate = jax.nn.sigmoid(gate_pre)
    silu_gate = gate_pre * sigmoid_gate
    activation = (silu_gate * up_pre).astype(jnp.bfloat16)
    grad_amax = lax.pmax(jnp.max(jnp.abs(grad_hidden)), "tensor")
    columns = slot_rows
    weight_sum = lax.psum_scatter(
        lax.dot_general(
            columns, activation, (((0,), (0,)), ((), ())), preferred_element_type=jnp.float32
        ).astype(jnp.bfloat16),
        "dp",
        scatter_dimension=0,
        tiled=True,
    )
    quantized = lax.optimization_barrier(
        (grad_hidden / (grad_amax + epsilon)).astype(jnp.bfloat16)
    ).astype(jnp.float32)
    grad_gate = (
        quantized * up_pre * sigmoid_gate * (1.0 + gate_pre * (1.0 - sigmoid_gate))
    ).astype(jnp.bfloat16)
    grad_up = (quantized * silu_gate).astype(jnp.bfloat16)
    weight_grad = weight_sum.reshape(w_down.shape)
    return (weight_grad, grad_gate, grad_up, grad_amax.reshape(1, 1))


def solution(mesh):
    placed = (
        P(("dp", "expert"), "tensor"),
        P(("dp", "expert"), None),
        P(("dp", "expert"), None),
        P("expert", "dp", "tensor"),
        P(("dp", "expert"), "tensor"),
        P(("dp", "expert"), "tensor"),
    )
    return jax.shard_map(
        body,
        mesh=mesh,
        in_specs=placed,
        out_specs=(
            P("expert", "dp", "tensor"),
            P(("dp", "expert"), "tensor"),
            P(("dp", "expert"), "tensor"),
            P("dp", "expert"),
        ),
        check_vma=False,
    )
```

profile of v0, /device:TPU:1, one launch (start us, length us, event | category | flops | bytes accessed | tf_op | source)
XLA Modules:
  0.0 214.2 jit_solution(183968141985197217)
XLA Ops:
  7.2 0.7 fusion.14
  7.9 0.1 copy.14
  8.0 0.2 reduce_window_sum.11
  8.2 0.1 copy.16
  8.3 0.1 copy.15
  8.4 1.2 select_reduce_fusion.2
  9.6 0.1 reshape.60
  9.7 9.1 %all_gather.6 = bf16[128,3584]{1,0:T(8,128)(2,1)S(1)} all-gather(bf16[128,1792]{1,0:T(8,128)(2,1)} %param.6), channel_id=1, replica_groups=mesh['dp'=4,'expert'=64,'tensor'=2] {'tensor'}, dimensions={1}, use_global_device_ids=true | all-gather | bytes 1376256 | tf_op jit(solution)/shard_map/all_gather | solution.py:29
  18.8 0.7 select_reduce_fusion.1
  19.6 0.1 select_reduce_fusion
  19.7 4.2 %gather_fusion = bf16[512,3584]{1,0:T(8,128)(2,1)} fusion(bf16[128,3584]{1,0:T(8,128)(2,1)S(1)} %all_gather.6, s32[1024]{0:T(1024)S(1)} %pad_clamp_fusion), kind=kCustom, calls=%fused_computation | custom fusion | bytes 7342080 | tf_op jit(solution)/shard_map/jit(_take)/gather | solution.py:30
  23.9 6.0 %multiply_convert_fusion = bf16[64,8,3584]{2,1,0:T(8,128)(2,1)} fusion(bf16[512,3584]{1,0:T(8,128)(2,1)} %gather_fusion, f32[64,8]{1,0:T(8,128)S(1)} %select_reduce_fusion, pred[64,8]{1,0:T(8,128)(4,1)S(1)} %compare_and_fusion), kind=kLoop, calls=%fused_computation.1 | loop fusion | flops 7340032 | bytes 7342592 | tf_op jit(solution)/shard_map/convert_element_type | solution.py:32
  29.9 0.0 copy-start
  29.9 0.0 copy-start.1
  29.9 11.3 %all-to-all-start = ((bf16[64,8,3584]{2,1,0:T(8,128)(2,1)}), bf16[64,8,3584]{2,1,0:T(8,128)(2,1)}, u32[]{:S(2)}, u32[]{:S(2)}) async-start(bf16[64,8,3584]{2,1,0:T(8,128)(2,1)} %multiply_convert_fusion), calls=%async_computation | async-start | bytes 7340032 | tf_op jit(solution)/shard_map/all_to_all | solution.py:31
  41.3 0.0 all-gather.2.cloned.1.call-start
  41.3 0.7 all-gather.2.cloned.1.call-update
  42.0 0.0 reduce-scatter.2.cloned.1.call-start
  42.1 86.3 %all-to-all-done = bf16[64,8,3584]{2,1,0:T(8,128)(2,1)} async-done(((bf16[64,8,3584]{2,1,0:T(8,128)(2,1)}), bf16[64,8,3584]{2,1,0:T(8,128)(2,1)}, u32[]{:S(2)}, u32[]{:S(2)}) %all-to-all-start) | async-done | bytes 3670048 | tf_op jit(solution)/shard_map/all_to_all | solution.py:31
  128.4 0.0 copy-done
  128.4 0.0 copy-done.1
  128.4 6.2 %convolution_convert_fusion = bf16[3584,512]{1,0:T(8,128)(2,1)} fusion(bf16[64,8,3584]{2,1,0:T(8,128)(2,1)} %all-to-all-done, bf16[512,512]{1,0:T(8,128)(2,1)S(1)} %copy-done, bf16[512,512]{1,0:T(8,128)(2,1)S(1)} %copy-done.1), kind=kOutput, calls=%fused_computation.2 | convolution fusion | flops 1882980352 | bytes 8388608 | tf_op jit(solution)/shard_map/dot_general | solution.py:53
  134.5 0.0 reduce-scatter.2.cloned.1.call-update
  134.6 0.0 all-gather.2.cloned.1.call-done
  134.6 5.9 %abs_reduce_fusion = (f32[]{:T(128)}, f32[512,512]{1,0:T(8,128)S(1)}) fusion(bf16[1,3584,512]{2,1,0:T(8,128)(2,1)} %all-gather.2.cloned.1.call-done, bf16[64,8,3584]{2,1,0:T(8,128)(2,1)} %all-to-all-done), kind=kOutput, calls=%fused_computation.24 | convolution fusion | flops 1879572480 | bytes 8388612 | tf_op jit(solution)/shard_map/dot_general | solution.py:40
  140.4 6.4 %pmax.7 = f32[]{:T(128)} all-reduce(f32[]{:T(128)} %get-tuple-element.8), channel_id=1, replica_groups=mesh['dp'=4,'expert'=64,'tensor'=2] {'tensor'}, use_global_device_ids=true, to_apply=%region_7.8 | all-reduce | flops 1 | bytes 8 | tf_op jit(solution)/shard_map/pmax | solution.py:50
  147.5 0.1 divide_convert_fusion
  147.7 1.5 fusion.8
  149.2 58.2 %reduce-scatter.2.cloned.1.call-done = bf16[896,512]{1,0:T(8,128)(2,1)} async-done(((bf16[3584,512]{1,0:T(8,128)(2,1)}), bf16[896,512]{1,0:T(8,128)(2,1)}) %reduce-scatter.2.cloned.1.call-update) | async-done | bytes 917520 | tf_op jit(solution)/shard_map/reduce_scatter | solution.py:52
  (5 shorter events, 0.1 us)
Async XLA Ops:
  29.9 98.4 %copy-start = (bf16[512,512]{1,0:T(8,128)(2,1)S(1)}, bf16[512,512]{1,0:T(8,128)(2,1)}, u32[]{:S(2)}) copy-start(bf16[512,512]{1,0:T(8,128)(2,1)} %param.11) | copy-start | bytes 1572868
  29.9 98.4 %copy-start.1 = (bf16[512,512]{1,0:T(8,128)(2,1)S(1)}, bf16[512,512]{1,0:T(8,128)(2,1)}, u32[]{:S(2)}) copy-start(bf16[512,512]{1,0:T(8,128)(2,1)} %param.10) | copy-start | bytes 1572868
  29.9 98.4 %all-to-all-start = ((bf16[64,8,3584]{2,1,0:T(8,128)(2,1)}), bf16[64,8,3584]{2,1,0:T(8,128)(2,1)}, u32[]{:S(2)}, u32[]{:S(2)}) async-start(bf16[64,8,3584]{2,1,0:T(8,128)(2,1)} %multiply_convert_fusion), calls=%async_computation | async-start | bytes 7340032 | tf_op jit(solution)/shard_map/all_to_all | solution.py:31
  41.3 93.3 %all-gather.2.cloned.1.call-start = ((), (), s32[]{:S(2)}) async-start(), calls=%async_computation.3 | async-start | bytes 4587520 | tf_op jit(solution)/shard_map/all_gather | solution.py:42
  42.0 165.3 %reduce-scatter.2.cloned.1.call-start = ((), (), s32[]{:S(2)}) async-start(), calls=%async_computation.2 | async-start | bytes 4587520 | tf_op jit(solution)/shard_map/reduce_scatter | solution.py:52
Sparse Core Ops, SparseCore 0:
  44.2 49.6 all-gather.1
  134.7 72.6 reduce-scatter.1
where the time goes:
time: 215 us; the launch traced here: 214 us
  waiting for transfers between devices  145 us (67%)
  blocking collectives  15.6 us (7%)
  between operations  14.8 us (7%)
  matrix products  12 us (6%)
  starting transfers between devices  11.4 us (5%)
  other arithmetic  10.7 us (5%)
  local copies, waits for them, and re-layouts  4.57 us (2%)
    all_to_all x1, waiting for transfers between devices, body(): lax.all_to_all((picked_rows.astype(jnp.float32) * slot_scale[:, :, None])...  86.3 us
    reduce_scatter x1, waiting for transfers between devices, body(): lax.psum_scatter(lax.dot_general(columns, activation, (((0,), (0,)), ((),...  58.2 us
    all_to_all x1, starting transfers between devices, body(): lax.all_to_all((picked_rows.astype(jnp.float32) * slot_scale[:, :, None])...  11.3 us
    all_gather x1, blocking collectives, body(): features = lax.all_gather(out_grad, 'tensor', axis=1, tiled=True)  9.14 us
    pmax x1, blocking collectives, body(): grad_amax = lax.pmax(jnp.max(jnp.abs(grad_hidden)), 'tensor')  6.43 us
    dot_general x1, matrix products, body(): lax.dot_general(columns, activation, (((0,), (0,)), ((), ())), preferred_...  6.16 us
    convert_element_type x1, other arithmetic, body(): (picked_rows.astype(jnp.float32) * slot_scale[:, :, None]).astype(jnp.bfl...  6.03 us
    dot_general x1, matrix products, body(): jnp.dot(columns, lax.all_gather(w_down, 'dp', axis=1, tiled=True)[0], pre...  5.85 us
  transfers between devices with their start and end apart: 3, of which 2 were waited for; matrix products, arithmetic and copies ran while one was open for 6% of the time, Pallas kernels for 0%

commit v1 on v0

v1 whole, which is shorter than its diff:
```python
import functools
import math

import jax
import jax.numpy as jnp
from jax import lax
from jax.experimental import pallas as pl
from jax.experimental.pallas import tpu as pltpu
from jax.sharding import PartitionSpec as P

MESH = pl.DeviceIdType.MESH
EPSILON = 1e-6
F32 = jnp.float32
BF16 = jnp.bfloat16


def kernel(
    nz, ny, og, ids, probs, w, gate, up,
    wg_out, gg_out, gu_out, amax_out,
    gv, uv, wv, a1, a2, tok, idb, prb, keyb, scb, S, X, act,
    gh, wacc, far_out, far_in, near_out, near_in, mx_out, mx_in,
    loc_sem, id_send, id_recv, pr_send, pr_recv, tok_send, tok_recv, tokf_send,
    act_send, act_recv, actf_send, actf_recv,
    a2a_send, a2a_recv, fwd_send, fwd_recv,
    far_send, far_recv, near_send, near_recv, mx_send, mx_recv,
):
    q = lax.axis_index("dp")
    e = lax.axis_index("expert")
    t = lax.axis_index("tensor")
    z = e // ny
    y = lax.rem(e, ny)
    half = nz // 2
    ne = nz * ny
    tokens, dc = tok.shape[1], tok.shape[2]
    top = ids.shape[0]
    cap = S.shape[3]
    slots, fh = gate.shape
    sh = slots // 2
    right, opposite, left = lax.rem(q + 1, 4), lax.rem(q + 2, 4), lax.rem(q + 3, 4)
    partner = (q, e, 1 - t)

    def rcopy(src, dst, ss, rs, dev):
        return pltpu.make_async_remote_copy(
            src_ref=src, dst_ref=dst, send_sem=ss, recv_sem=rs, device_id=dev, device_id_type=MESH
        )

    copy_g = pltpu.make_async_copy(gate, gv, loc_sem.at[0])
    copy_u = pltpu.make_async_copy(up, uv, loc_sem.at[1])
    copy_w = pltpu.make_async_copy(w, wv, loc_sem.at[2])
    copy_g.start()
    copy_u.start()
    copy_w.start()

    barrier = pltpu.get_barrier_semaphore()
    for r in range(1, 4):
        pl.semaphore_signal(barrier, inc=1, device_id=(lax.rem(q + r, 4), e, t), device_id_type=MESH)
    pl.semaphore_signal(barrier, inc=1, device_id=partner, device_id_type=MESH)

    def greet(n, carry):
        dz, dy = 2 * (n // ny) + t, lax.rem(n, ny)
        peer = lax.rem(z + dz, nz) * ny + lax.rem(y + dy, ny)

        @pl.when(dz + dy > 0)
        def _():
            pl.semaphore_signal(barrier, inc=1, device_id=(q, peer, t), device_id_type=MESH)

        return carry

    lax.fori_loop(0, half * ny, greet, 0)

    copy_g.wait()
    copy_u.wait()
    rows = slots // nz

    def activate(n, carry):
        at = pl.ds(pl.multiple_of(n * rows, rows), rows)
        g = gv[at, :].astype(F32)
        u = uv[at, :].astype(F32)
        s = jax.nn.sigmoid(g)
        silu = g * s
        act[0, at, :] = (silu * u).astype(BF16)
        a1[at, :] = u * s * (1.0 + g * (1.0 - s))
        a2[at, :] = silu
        return carry

    lax.fori_loop(0, nz, activate, 0)

    def make_key(r, id_rows, pr_rows):
        owner = lax.broadcasted_iota(jnp.int32, (ne, tokens), 0)
        routed = jnp.zeros((ne, tokens), F32)
        scale = jnp.zeros((ne, tokens), F32)
        for k in range(top):
            match = owner == id_rows[k : k + 1, :]
            routed = jnp.where(match, 1.0, routed)
            scale = scale + jnp.where(match, pr_rows[k : k + 1, :], 0.0)
        before = lax.broadcasted_iota(jnp.int32, (tokens, tokens), 0)
        after = lax.broadcasted_iota(jnp.int32, (tokens, tokens), 1)
        upper = jnp.where(before < after, 1.0, 0.0).astype(BF16)
        rank = jnp.dot(routed.astype(BF16), upper, preferred_element_type=F32)
        keyb[r] = jnp.where(routed > 0.0, rank, -1.0)
        scb[r] = scale

    make_key(0, ids[...], probs[...])

    pl.semaphore_wait(barrier, half * ny + 3 + t)

    for j in range(2):
        dest = 2 * t + j
        source = og.at[:, pl.ds(j * dc, dc)]

        @pl.when(dest != q)
        def _():
            slot = lax.rem(q - dest + 4, 4)
            rcopy(source, tok.at[slot], tok_send.at[j], tok_recv.at[slot], (dest, e, t)).start()

        @pl.when(dest == q)
        def _():
            pltpu.make_async_copy(source, tok.at[0], tok_recv.at[0]).start()
            rcopy(source, tok.at[0], tokf_send.at[0], tok_recv.at[0], partner).start()

    for r in (2, 1, 3):
        peer = (lax.rem(q + r, 4), e, t)
        slot = (4 - r) % 4
        rcopy(ids, idb.at[slot], id_send.at[r], id_recv.at[slot], peer).start()
        rcopy(probs, prb.at[slot], pr_send.at[r], pr_recv.at[slot], peer).start()
    rcopy(act.at[0], act.at[3], act_send.at[0], act_recv.at[0], (right, e, t)).start()
    rcopy(act.at[0], act.at[1], act_send.at[1], act_recv.at[1], (left, e, t)).start()

    holder = lax.div(q, 2) == t

    def get_tokens(r):
        rcopy(tok.at[r], tok.at[r], tokf_send.at[r], tok_recv.at[r], partner).wait_recv()
        if r > 0:

            @pl.when(holder)
            def _():
                rcopy(tok.at[r], tok.at[r], tokf_send.at[r], tok_recv.at[r], partner).start()

            rcopy(ids, idb.at[r], id_send.at[r], id_recv.at[r], partner).wait_recv()
            rcopy(probs, prb.at[r], pr_send.at[r], pr_recv.at[r], partner).wait_recv()
            make_key(r, idb[r], prb[r])

    rank_of = lax.broadcasted_iota(jnp.int32, (cap, tokens), 0).astype(F32)

    def send_rows(r, first, last):
        def build(i):
            zz = lax.rem(z + 2 * i + t, nz)
            at = pl.ds(pl.multiple_of(zz * ny, ny), ny)
            keys, scales = keyb[r, at, :], scb[r, at, :]
            picks, weights = [], []
            for yy in range(ny):
                hit = keys[yy : yy + 1, :] == rank_of
                picks.append(jnp.where(hit, 1.0, 0.0))
                weights.append(jnp.sum(jnp.where(hit, scales[yy : yy + 1, :], 0.0), axis=1, keepdims=True))
            pick = jnp.concatenate(picks, axis=0).astype(BF16)
            weight = jnp.concatenate(weights, axis=0)
            value = jnp.dot(pick, tok[r], preferred_element_type=F32) * weight
            for yy in range(ny):
                S[r, zz, yy] = value[yy * cap : (yy + 1) * cap, :].astype(BF16)

        def send(i):
            dz = 2 * i + t
            zz = lax.rem(z + dz, nz)

            def one(dy, carry):
                yy = lax.rem(y + dy, ny)

                @pl.when(dz + dy > 0)
                def _():
                    rcopy(
                        S.at[r, zz, yy], X.at[r, z, y], a2a_send.at[r, i], a2a_recv.at[r, i], (q, zz * ny + yy, t)
                    ).start()

                @pl.when(dz + dy == 0)
                def _():
                    pltpu.make_async_copy(S.at[r, zz, yy], X.at[r, z, y], a2a_recv.at[r, i]).start()

                return carry

            lax.fori_loop(0, ny, one, 0)

        build(first)

        def step(i, carry):
            build(i)
            send(i - 1)
            return carry

        lax.fori_loop(first + 1, last, step, 0)
        return lambda: send(last - 1)

    split = max(1, half // 2)
    get_tokens(0)
    finish = send_rows(0, 0, split)
    get_tokens(2)
    finish()
    finish = send_rows(2, 0, half)
    get_tokens(1)
    finish()
    finish = send_rows(1, 0, half)
    get_tokens(3)
    finish()
    finish = send_rows(3, 0, half)
    rcopy(act.at[0], act.at[3], act_send.at[0], act_recv.at[0], (right, e, t)).wait_recv()
    low, high = pl.ds(0, sh), pl.ds(sh, sh)
    rcopy(act.at[3, low], act.at[2, low], actf_send.at[0], actf_recv.at[0], (right, e, t)).start()
    rcopy(act.at[0], act.at[1], act_send.at[1], act_recv.at[1], (left, e, t)).wait_recv()
    rcopy(act.at[1, high], act.at[2, high], actf_send.at[1], actf_recv.at[1], (left, e, t)).start()
    finish()
    if split < half:
        finish = send_rows(0, split, half)
    else:
        finish = lambda: None

    def arrive(r, first, last):
        def step(i, carry):
            zs = lax.rem(z - (2 * i + t) + nz, nz)
            block = X.at[r, zs]
            rcopy(block, block, fwd_send.at[r, i], a2a_recv.at[r, i], partner).wait_recv()
            rcopy(block, block, fwd_send.at[r, i], fwd_recv.at[r, i], partner).start()
            return carry

        lax.fori_loop(first, last, step, 0)

    def arrive_partner(r):
        def step(i, carry):
            zs = lax.rem(z - (2 * i + 1 - t) + nz, nz)
            block = X.at[r, zs]
            rcopy(block, block, fwd_send.at[r, i], fwd_recv.at[r, i], partner).wait_recv()
            return carry

        lax.fori_loop(0, half, step, 0)

    def grad_hidden(r):
        for h in range(2):
            block = X[r, h * half : (h + 1) * half].reshape(sh, dc)
            gh[h * sh : (h + 1) * sh, :] = jnp.dot(block, wv[...], preferred_element_type=F32)

    def weight_grad(r, init):
        step = 128

        def body(n, carry):
            at = pl.ds(pl.multiple_of(n * step, step), step)
            block = X[r, :, :, :, at].reshape(slots, step)
            value = lax.dot_general(block, act[r], (((0,), (0,)), ((), ())), preferred_element_type=F32)
            if init:
                wacc[at, :] = value
            else:
                wacc[at, :] += value
            return carry

        lax.fori_loop(0, dc // step, body, 0)

    arrive(0, 0, split)
    finish()
    copy_w.wait()

    arrive(2, 0, half)
    arrive_partner(2)
    grad_hidden(2)
    far_out[...] = gh[...].astype(BF16)
    rcopy(act.at[3, low], act.at[2, low], actf_send.at[0], actf_recv.at[0], (right, e, t)).wait_recv()
    rcopy(act.at[1, high], act.at[2, high], actf_send.at[1], actf_recv.at[1], (left, e, t)).wait_recv()
    rcopy(far_out.at[low], far_in.at[0], far_send.at[0], far_recv.at[0], (right, e, t)).start()
    rcopy(far_out.at[high], far_in.at[1], far_send.at[1], far_recv.at[1], (left, e, t)).start()
    weight_grad(2, True)

    for n, (r, dest, part) in enumerate(((1, right, low), (3, left, high))):
        arrive(r, 0, half)
        arrive_partner(r)
        grad_hidden(r)
        rcopy(far_out.at[part], far_in.at[n], far_send.at[n], far_recv.at[n], (dest, e, t)).wait_recv()
        gh[part, :] += far_in[n].astype(F32)
        near_out[n] = gh[...].astype(BF16)
        weight_grad(r, False)
        rcopy(near_out.at[n], near_in.at[n], near_send.at[n], near_recv.at[n], (dest, e, t)).start()

    arrive(0, split, half)
    arrive_partner(0)
    grad_hidden(0)
    for n, dest in ((0, right), (1, left)):
        rcopy(near_out.at[n], near_in.at[n], near_send.at[n], near_recv.at[n], (dest, e, t)).wait_recv()

    def total(n, largest):
        at = pl.ds(pl.multiple_of(n * rows, rows), rows)
        value = gh[at, :] + near_in[0, at, :].astype(F32) + near_in[1, at, :].astype(F32)
        gh[at, :] = value
        return jnp.maximum(largest, jnp.max(jnp.abs(value)))

    largest = lax.fori_loop(0, nz, total, jnp.zeros((), F32))
    mx_out[...] = jnp.full(mx_out.shape, largest, F32)
    weight_grad(0, False)
    exchange = rcopy(mx_out, mx_in, mx_send.at[0], mx_recv.at[0], partner)
    exchange.start()
    wg_out[...] = wacc[...].astype(BF16)
    exchange.wait_recv()
    amax = jnp.maximum(mx_out[...], mx_in[...])
    amax_out[...] = amax
    inverse = 1.0 / (amax[0:1, 0:1] + EPSILON)

    def scale_out(n, carry):
        at = pl.ds(pl.multiple_of(n * rows, rows), rows)
        quantized = (gh[at, :] * inverse).astype(BF16).astype(F32)
        gg_out[at, :] = (quantized * a1[at, :]).astype(BF16)
        gu_out[at, :] = (quantized * a2[at, :]).astype(BF16)
        return carry

    lax.fori_loop(0, nz, scale_out, 0)

    for j in range(2):
        source = og.at[:, pl.ds(j * dc, dc)]

        @pl.when(2 * t + j != q)
        def _():
            rcopy(source, tok.at[0], tok_send.at[j], tok_recv.at[0], partner).wait_send()

        @pl.when(2 * t + j == q)
        def _():
            rcopy(source, tok.at[0], tokf_send.at[0], tok_recv.at[0], partner).wait_send()

    for r in range(1, 4):

        @pl.when(holder)
        def _():
            rcopy(tok.at[r], tok.at[r], tokf_send.at[r], tok_recv.at[r], partner).wait_send()

        rcopy(ids, idb.at[r], id_send.at[r], id_recv.at[r], partner).wait_send()
        rcopy(probs, prb.at[r], pr_send.at[r], pr_recv.at[r], partner).wait_send()
    for n in range(2):
        rcopy(act.at[0], act.at[1], act_send.at[n], act_recv.at[n], partner).wait_send()
        rcopy(act.at[1, low], act.at[2, low], actf_send.at[n], actf_recv.at[n], partner).wait_send()
        rcopy(far_out.at[low], far_in.at[n], far_send.at[n], far_recv.at[n], partner).wait_send()
        rcopy(near_out.at[n], near_in.at[n], near_send.at[n], near_recv.at[n], partner).wait_send()
    exchange.wait_send()
    for r in range(4):

        def drain(i, carry):
            block = X.at[r, 0]
            rcopy(block, block, fwd_send.at[r, i], fwd_recv.at[r, i], partner).wait_send()

            @pl.when(i + t > 0)
            def _():
                rcopy(S.at[r, 0], block, a2a_send.at[r, i], a2a_recv.at[r, i], partner).wait_send()

            @pl.when(i + t == 0)
            def _():
                some = pl.ds(0, ny - 1)
                rcopy(
                    S.at[r, 0, some], X.at[r, 0, some], a2a_send.at[r, i], a2a_recv.at[r, i], partner
                ).wait_send()

            return carry

        lax.fori_loop(0, half, drain, 0)


def body(side, out_grad, routing, route_probs, w_down, saved_gate, saved_up):
    nz = ny = side
    tokens, wide = out_grad.shape
    _, dc, fh = w_down.shape
    slots = saved_gate.shape[0]
    cap = slots // (nz * ny)
    top = routing.shape[1]
    half = nz // 2
    dma = pltpu.SemaphoreType.DMA
    scratch = [
        pltpu.VMEM((slots, fh), BF16),
        pltpu.VMEM((slots, fh), BF16),
        pltpu.VMEM((dc, fh), BF16),
        pltpu.VMEM((slots, fh), F32),
        pltpu.VMEM((slots, fh), F32),
        pltpu.VMEM((4, tokens, dc), BF16),
        pltpu.VMEM((4, top, tokens), jnp.int32),
        pltpu.VMEM((4, top, tokens), F32),
        pltpu.VMEM((4, nz * ny, tokens), F32),
        pltpu.VMEM((4, nz * ny, tokens), F32),
        pltpu.VMEM((4, nz, ny, cap, dc), BF16),
        pltpu.VMEM((4, nz, ny, cap, dc), BF16),
        pltpu.VMEM((4, slots, fh), BF16),
        pltpu.VMEM((slots, fh), F32),
        pltpu.VMEM((dc, fh), F32),
        pltpu.VMEM((slots, fh), BF16),
        pltpu.VMEM((2, slots // 2, fh), BF16),
        pltpu.VMEM((2, slots, fh), BF16),
        pltpu.VMEM((2, slots, fh), BF16),
        pltpu.VMEM((8, 128), F32),
        pltpu.VMEM((8, 128), F32),
        dma((3,)),
        dma((4,)), dma((4,)), dma((4,)), dma((4,)),
        dma((2,)), dma((4,)), dma((4,)),
        dma((2,)), dma((2,)), dma((2,)), dma((2,)),
        dma((4, half)), dma((4, half)), dma((4, half)), dma((4, half)),
        dma((2,)), dma((2,)), dma((2,)), dma((2,)), dma((1,)), dma((1,)),
    ]
    vmem = pl.BlockSpec(memory_space=pltpu.VMEM)
    anywhere = pl.BlockSpec(memory_space=pl.ANY)
    wg, gg, gu, amax = pl.pallas_call(
        functools.partial(kernel, nz, ny),
        out_shape=(
            jax.ShapeDtypeStruct((dc, fh), BF16),
            jax.ShapeDtypeStruct((slots, fh), BF16),
            jax.ShapeDtypeStruct((slots, fh), BF16),
            jax.ShapeDtypeStruct((8, 128), F32),
        ),
        in_specs=[anywhere, vmem, vmem, anywhere, anywhere, anywhere],
        out_specs=(vmem,) * 4,
        scratch_shapes=scratch,
        compiler_params=pltpu.CompilerParams(
            collective_id=0, has_side_effects=True, vmem_limit_bytes=56 * 1024 * 1024
        ),
    )(out_grad, routing.T, route_probs.T, w_down[0], saved_gate, saved_up)
    return wg.reshape(w_down.shape), gg, gu, amax[0:1, 0:1]


def solution(mesh):
    placed = (
        P(("dp", "expert"), "tensor"),
        P(("dp", "expert"), None),
        P(("dp", "expert"), None),
        P("expert", "dp", "tensor"),
        P(("dp", "expert"), "tensor"),
        P(("dp", "expert"), "tensor"),
    )
    return jax.shard_map(
        functools.partial(body, math.isqrt(mesh.shape["expert"])),
        mesh=mesh,
        in_specs=placed,
        out_specs=(
            P("expert", "dp", "tensor"),
            P(("dp", "expert"), "tensor"),
            P(("dp", "expert"), "tensor"),
            P("dp", "expert"),
        ),
        check_vma=False,
    )
```

time: 215 us -> 113 us (0.53)
  waiting for transfers between devices: 145 us -> 0 us
  Pallas kernels: 0 us -> 107 us
  blocking collectives: 15.6 us -> 0 us
  between operations: 14.8 us -> 0.64 us
  matrix products: 12 us -> 0 us
  starting transfers between devices: 11.4 us -> 0 us
  other arithmetic: 10.7 us -> 0 us
    pallas_call x0 -> x1, Pallas kernels: none -> 107 us  [body(): pl.pallas_call(functools.partial(kernel, nz, ny), out_shape=(jax.ShapeDty...]
    all_to_all x1 -> x0, waiting for transfers between devices: 86.3 us -> none  [body(): lax.all_to_all((picked_rows.astype(jnp.float32) * slot_scale[:, :, None])...]
    reduce_scatter x1 -> x0, waiting for transfers between devices: 58.2 us -> none  [body(): lax.psum_scatter(lax.dot_general(columns, activation, (((0,), (0,)), ((),...]
    dot_general x2 -> x0, matrix products: 12 us -> none  [the longest x1 6.16 us: body(): lax.dot_general(columns, activation, (((0,), (0,)), ((), ())), preferred_...]
    all_to_all x1 -> x0, starting transfers between devices: 11.3 us -> none  [body(): lax.all_to_all((picked_rows.astype(jnp.float32) * slot_scale[:, :, None])...]
    all_gather x1 -> x0, blocking collectives: 9.14 us -> none  [body(): features = lax.all_gather(out_grad, 'tensor', axis=1, tiled=True)]
    convert_element_type x3 -> x0, other arithmetic: 7.67 us -> none  [the longest x1 6.03 us: body(): (picked_rows.astype(jnp.float32) * slot_scale[:, :, None]).astype(jnp.bfl...]
    pmax x1 -> x0, blocking collectives: 6.43 us -> none  [body(): grad_amax = lax.pmax(jnp.max(jnp.abs(grad_hidden)), 'tensor')]
  transfers between devices with their start and end apart: 3 -> 0, of which waited for: 2 -> 0; matrix products, arithmetic and copies ran while one was open for 6% -> 0% of each run, Pallas kernels for 0% -> 0%
where the time goes in v1:
time: 113 us
  Pallas kernels  107 us (95%)
  local copies, waits for them, and re-layouts  5.43 us (5%)
    pallas_call x1, Pallas kernels, body(): pl.pallas_call(functools.partial(kernel, nz, ny), out_shape=(jax.ShapeDty...  107 us
    unnamed x7, local copies, waits for them, and re-layouts  4.24 us

profile of v1, /device:TPU:1, one launch (start us, length us, event | category | flops | bytes accessed | tf_op | source)
XLA Modules:
  0.0 112.8 jit_solution(402854943048204017)
XLA Ops:
  0.6 106.7 %shard_map.93 = (bf16[896,512]{1,0:T(8,128)(2,1)}, bf16[512,512]{1,0:T(8,128)(2,1)}, bf16[512,512]{1,0:T(8,128)(2,1)}, f32[8,128]{1,0:T(8,128)}) custom-call(bf16[128,1792]{1,0:T(8,128)(2,1)} %og.1, s32[8,128]{1,0:T(8,128)} %bitcast.6, f32[8,128]{1,0:T(8,128)} %bitcast.7, bf16[896,512]{1,0:T(8,128)(2,1)} %bitcast.5, bf16[512,512]{1,0:T(8,128)(2,1)} %gate.1, ...), custom_call_target="tpu_custom_call" | custom-call | tf_op jit(solution)/shard_map/pallas_call | solution.py:397
  107.4 1.2 %slice.3 = f32[1,1]{1,0:T(1,128)} slice(f32[8,128]{1,0:T(8,128)} %get-tuple-element.11), slice={[0:1], [0:1]} | slice | bytes 8 | tf_op jit(solution)/shard_map/slice | solution.py:412
  108.6 0.0 copy-start.1
  108.6 2.2 %copy.13 = bf16[1,896,512]{2,1,0:T(8,128)(2,1)} copy(bf16[1,896,512]{2,1,0:T(8,128)(2,1)} %bitcast.4) | data formatting | bytes 1835008
  110.8 0.0 copy-done.1
  110.8 0.0 copy-start
  110.8 0.8 copy.14
  111.6 0.4 copy-done
  112.0 0.8 copy.15
Async XLA Ops:
  108.6 2.2 %copy-start.1 = (bf16[512,512]{1,0:T(8,128)(2,1)S(1)}, bf16[512,512]{1,0:T(8,128)(2,1)}, u32[]{:S(2)}) copy-start(bf16[512,512]{1,0:T(8,128)(2,1)} %get-tuple-element.17) | copy-start | bytes 1572868
  110.8 1.2 %copy-start = (bf16[512,512]{1,0:T(8,128)(2,1)S(1)}, bf16[512,512]{1,0:T(8,128)(2,1)}, u32[]{:S(2)}) copy-start(bf16[512,512]{1,0:T(8,128)(2,1)} %get-tuple-element.18) | copy-start | bytes 1572868

commit v2 on v1

v2 whole, which is shorter than its diff:
```python
import functools
import math

import jax
import jax.numpy as jnp
from jax import lax
from jax.experimental import pallas as pl
from jax.experimental.pallas import tpu as pltpu
from jax.sharding import PartitionSpec as P

MESH = pl.DeviceIdType.MESH
EPSILON = 1e-6
F32 = jnp.float32
BF16 = jnp.bfloat16


def kernel(
    nz, ny, og, ids, probs, w, gate, up,
    wg_out, gg_out, gu_out, amax_out,
    gv, uv, wv, a1, a2, tok, idb, prb, keyb, scb, S, X, act,
    gh, wacc, far_out, far_in, near_out, near_in, mx_out, mx_in,
    loc_sem, id_send, id_recv, pr_send, pr_recv, tok_send, tok_recv, tokf_send,
    act_send, act_recv, actf_send, actf_recv,
    a2a_send, a2a_recv, fwd_send, fwd_recv,
    far_send, far_recv, near_send, near_recv, mx_send, mx_recv,
):
    q = lax.axis_index("dp")
    e = lax.axis_index("expert")
    t = lax.axis_index("tensor")
    z = e // ny
    y = lax.rem(e, ny)
    half = nz // 2
    ne = nz * ny
    tokens, dc = tok.shape[1], tok.shape[2]
    top = ids.shape[0]
    cap = S.shape[3]
    lag = 3
    slots, fh = gate.shape
    sh = slots // 2
    right, opposite, left = lax.rem(q + 1, 4), lax.rem(q + 2, 4), lax.rem(q + 3, 4)
    partner = (q, e, 1 - t)

    def rcopy(src, dst, ss, rs, dev):
        return pltpu.make_async_remote_copy(
            src_ref=src, dst_ref=dst, send_sem=ss, recv_sem=rs, device_id=dev, device_id_type=MESH
        )

    copies = [
        pltpu.make_async_copy(source, target, loc_sem.at[n])
        for n, (source, target) in enumerate(((ids, idb.at[0]), (probs, prb.at[0]), (gate, gv), (up, uv), (w, wv)))
    ]
    for copy in copies:
        copy.start()

    barrier = pltpu.get_barrier_semaphore()

    def greet(n, carry):
        dz, dy = 2 * (n // ny) + t, lax.rem(n, ny)
        peer = lax.rem(z + dz, nz) * ny + lax.rem(y + dy, ny)

        @pl.when(dz + dy > 0)
        def _():
            pl.semaphore_signal(barrier, inc=1, device_id=(q, peer, t), device_id_type=MESH)

        return carry

    lax.fori_loop(0, half * ny, greet, 0)
    for r in range(1, 4):
        pl.semaphore_signal(barrier, inc=1, device_id=(lax.rem(q + r, 4), e, t), device_id_type=MESH)
    pl.semaphore_signal(barrier, inc=1, device_id=partner, device_id_type=MESH)

    rows = slots // nz

    def natural(n):
        return pl.ds(pl.multiple_of(lax.rem(z - n + nz, nz) * rows, rows), rows)

    def ordered(n):
        return pl.ds(pl.multiple_of(n * rows, rows), rows)

    def activate(n, carry):
        g = gv[natural(n), :].astype(F32)
        u = uv[natural(n), :].astype(F32)
        s = jax.nn.sigmoid(g)
        silu = g * s
        act[0, ordered(n), :] = (silu * u).astype(BF16)
        a1[ordered(n), :] = u * s * (1.0 + g * (1.0 - s))
        a2[ordered(n), :] = silu
        return carry

    copies[2].wait()
    copies[3].wait()
    lax.fori_loop(0, nz, activate, 0)

    def make_key(r):
        owner = lax.broadcasted_iota(jnp.int32, (ne, tokens), 0)
        routed = jnp.zeros((ne, tokens), F32)
        scale = jnp.zeros((ne, tokens), F32)
        for k in range(top):
            match = owner == idb[r, k : k + 1, :]
            routed = jnp.where(match, 1.0, routed)
            scale = scale + jnp.where(match, prb[r, k : k + 1, :], 0.0)
        before = lax.broadcasted_iota(jnp.int32, (tokens, tokens), 0)
        after = lax.broadcasted_iota(jnp.int32, (tokens, tokens), 1)
        upper = jnp.where(before < after, 1.0, 0.0).astype(BF16)
        rank = jnp.dot(routed.astype(BF16), upper, preferred_element_type=F32)
        keyb[r] = jnp.where(routed > 0.0, rank, -1.0)
        scb[r] = scale

    def token_chunk(n):
        j = lax.rem(q + n, 2)
        return 2 * t + j, og.at[:, pl.ds(pl.multiple_of(j * dc, 128), dc)]

    copies[0].wait()
    copies[1].wait()
    make_key(0)
    holder = lax.div(q, 2) == t

    @pl.when(holder)
    def _():
        pltpu.make_async_copy(token_chunk(0)[1], tok.at[0], tok_recv.at[0]).start()

    pl.semaphore_wait(barrier, half * ny + 3 + t)

    @pl.when(holder)
    def _():
        rcopy(token_chunk(0)[1], tok.at[0], tokf_send.at[0], tok_recv.at[0], partner).start()

    @pl.when(jnp.logical_not(holder))
    def _():
        dest, source = token_chunk(0)
        rcopy(source, tok.at[2], tok_send.at[0], tok_recv.at[2], (dest, e, t)).start()

    dest, source = token_chunk(1)
    slot = lax.rem(q - dest + 4, 4)
    rcopy(source, tok.at[slot], tok_send.at[1], tok_recv.at[slot], (dest, e, t)).start()
    for r in (2, 1, 3):
        peer = (lax.rem(q + r, 4), e, t)
        slot = (4 - r) % 4
        rcopy(ids, idb.at[slot], id_send.at[r], id_recv.at[slot], peer).start()
        rcopy(probs, prb.at[slot], pr_send.at[r], pr_recv.at[slot], peer).start()

    def get_tokens(r):
        if r > 0:
            rcopy(ids, idb.at[r], id_send.at[r], id_recv.at[r], partner).wait_recv()
            rcopy(probs, prb.at[r], pr_send.at[r], pr_recv.at[r], partner).wait_recv()
            make_key(r)
        rcopy(tok.at[r], tok.at[r], tokf_send.at[r], tok_recv.at[r], partner).wait_recv()
        if r > 0:

            @pl.when(holder)
            def _():
                rcopy(tok.at[r], tok.at[r], tokf_send.at[r], tok_recv.at[r], partner).start()

    rank_of = lax.broadcasted_iota(jnp.int32, (cap, tokens), 0).astype(F32)

    def build(r, i):
        zz = lax.rem(z + 2 * i + t, nz)
        at = pl.ds(pl.multiple_of(zz * ny, ny), ny)
        keys, scales = keyb[r, at, :], scb[r, at, :]
        picks, weights = [], []
        for yy in range(ny):
            hit = keys[yy : yy + 1, :] == rank_of
            picks.append(jnp.where(hit, 1.0, 0.0))
            weights.append(jnp.sum(jnp.where(hit, scales[yy : yy + 1, :], 0.0), axis=1, keepdims=True))
        pick = jnp.concatenate(picks, axis=0).astype(BF16)
        weight = jnp.concatenate(weights, axis=0)
        value = jnp.dot(pick, tok[r], preferred_element_type=F32) * weight
        for yy in range(ny):
            S[r, i, yy] = value[yy * cap : (yy + 1) * cap, :].astype(BF16)

    def send(r, i):
        dz = 2 * i + t
        zz = lax.rem(z + dz, nz)

        def one(k, carry):
            dy = lax.rem(jnp.where(lax.rem(k, 2) == 1, ny // 2 + (k + 1) // 2, ny // 2 - k // 2), ny)
            yy = lax.rem(y + dy, ny)
            row, target = S.at[r, i, yy], X.at[r, dz, y]

            @pl.when(dz + dy > 0)
            def _():
                rcopy(row, target, a2a_send.at[r, i], a2a_recv.at[r, i], (q, zz * ny + yy, t)).start()

            @pl.when(dz + dy == 0)
            def _():
                pltpu.make_async_copy(row, target, a2a_recv.at[r, i]).start()

            return carry

        lax.fori_loop(0, ny, one, 0)

    def arrive(r, i):
        block = X.at[r, 2 * i + t]
        rcopy(block, block, fwd_send.at[r, i], a2a_recv.at[r, i], partner).wait_recv()
        rcopy(block, block, fwd_send.at[r, i], fwd_recv.at[r, i], partner).start()

    def arrive_partner(r, i):
        block = X.at[r, 2 * i + 1 - t]
        rcopy(block, block, fwd_send.at[r, i], fwd_recv.at[r, i], partner).wait_recv()

    low, high = pl.ds(0, sh), pl.ds(sh, sh)
    parts = (low, high)

    def grad_hidden(r, h):
        block = X[r, h * half : (h + 1) * half].reshape(sh, dc)
        return jnp.dot(block, wv[...], preferred_element_type=F32)

    def weight_grad(r, init):
        step = 128

        def body(n, carry):
            at = pl.ds(pl.multiple_of(n * step, step), step)
            block = X[r, :, :, :, at].reshape(slots, step)
            value = lax.dot_general(block, act[r], (((0,), (0,)), ((), ())), preferred_element_type=F32)
            if init:
                wacc[at, :] = value
            else:
                wacc[at, :] += value
            return carry

        lax.fori_loop(0, dc // step, body, 0)

    def act_copy(n):
        dest, slot = ((right, 3), (left, 1))[n]
        return rcopy(act.at[0], act.at[slot], act_send.at[n], act_recv.at[n], (dest, e, t))

    def act_forward(n):
        dest, slot = ((right, 3), (left, 1))[n]
        return rcopy(act.at[slot, parts[n]], act.at[2, parts[n]], actf_send.at[n], actf_recv.at[n], (dest, e, t))

    def far_copy(n):
        dest = (right, left)[n]
        return rcopy(far_out.at[parts[n]], far_in.at[n], far_send.at[n], far_recv.at[n], (dest, e, t))

    def near_copy(n, h):
        dest = (right, left)[n]
        rows_h = parts[h]
        return rcopy(
            near_out.at[n, rows_h], near_in.at[n, rows_h], near_send.at[n, h], near_recv.at[n, h], (dest, e, t)
        )

    def hidden(r, h):
        value = grad_hidden(r, h)
        if r == 2:
            far_out[parts[h], :] = value.astype(BF16)
            far_copy(h).start()
        elif r == 0:
            gh[parts[h], :] = value
        else:
            n = 0 if r == 1 else 1
            if h == n:
                far_copy(n).wait_recv()
                value = value + far_in[n].astype(F32)
            near_out[n, parts[h], :] = value.astype(BF16)
            near_copy(n, h).start()

    last = max(1, half - 1)
    order = [(0, i) for i in range(last)]
    for r in (2, 1, 3):
        order += [(r, i) for i in range(half)]
    order += [(0, i) for i in range(last, half)]
    count = len(order)
    done = {}
    for k in range(count + lag + 1):
        if k < count:
            r, i = order[k]
            if i == 0:
                get_tokens(r)
            build(r, i)
            send(r, i)
        if k == last:
            act_copy(0).start()
            act_copy(1).start()
        if k == min(10, count):
            for n in range(2):
                act_copy(n).wait_recv()
                act_forward(n).start()
        if lag <= k < count + lag:
            arrive(*order[k - lag])
        if lag < k:
            r, i = order[k - lag - 1]
            arrive_partner(r, i)
            if k == lag + 1:
                copies[4].wait()
            if half == 1:
                hidden(r, 0)
                hidden(r, 1)
            elif i % (half // 2) == half // 2 - 1:
                hidden(r, i // (half // 2))
            if i == half - 1:
                if r == 1:
                    act_forward(0).wait_recv()
                    act_forward(1).wait_recv()
                    weight_grad(2, True)
                    weight_grad(1, False)
                elif r == 3:
                    weight_grad(3, False)
    assert order[-1][0] == 0 or half == 1
    for h in range(2):
        for n in range(2):
            near_copy(n, h).wait_recv()

    def total(n, largest):
        at = ordered(n)
        value = gh[at, :] + near_in[0, at, :].astype(F32) + near_in[1, at, :].astype(F32)
        gh[at, :] = value
        return jnp.maximum(largest, jnp.max(jnp.abs(value)))

    largest = lax.fori_loop(0, nz, total, jnp.zeros((), F32))
    mx_out[...] = jnp.full(mx_out.shape, largest, F32)
    exchange = rcopy(mx_out, mx_in, mx_send.at[0], mx_recv.at[0], partner)
    weight_grad(0, False)
    exchange.start()
    wg_out[...] = wacc[...].astype(BF16)
    exchange.wait_recv()
    amax = jnp.maximum(mx_out[...], mx_in[...])
    amax_out[...] = amax
    inverse = 1.0 / (amax[0:1, 0:1] + EPSILON)

    def scale_out(n, carry):
        at = ordered(n)
        quantized = (gh[at, :] * inverse).astype(BF16).astype(F32)
        gg_out[natural(n), :] = (quantized * a1[at, :]).astype(BF16)
        gu_out[natural(n), :] = (quantized * a2[at, :]).astype(BF16)
        return carry

    lax.fori_loop(0, nz, scale_out, 0)

    dest, source = token_chunk(1)
    rcopy(source, tok.at[0], tok_send.at[1], tok_recv.at[0], partner).wait_send()

    @pl.when(holder)
    def _():
        for r in range(4):
            rcopy(tok.at[r], tok.at[r], tokf_send.at[r], tok_recv.at[r], partner).wait_send()

    @pl.when(jnp.logical_not(holder))
    def _():
        rcopy(source, tok.at[0], tok_send.at[0], tok_recv.at[0], partner).wait_send()

    for r in range(1, 4):
        rcopy(ids, idb.at[r], id_send.at[r], id_recv.at[r], partner).wait_send()
        rcopy(probs, prb.at[r], pr_send.at[r], pr_recv.at[r], partner).wait_send()
    for n in range(2):
        act_copy(n).wait_send()
        act_forward(n).wait_send()
        far_copy(n).wait_send()
        for h in range(2):
            near_copy(n, h).wait_send()
    exchange.wait_send()
    for r in range(4):

        def drain(i, carry):
            block = X.at[r, 0]
            rcopy(block, block, fwd_send.at[r, i], fwd_recv.at[r, i], partner).wait_send()

            @pl.when(i + t > 0)
            def _():
                rcopy(S.at[r, 0], block, a2a_send.at[r, i], a2a_recv.at[r, i], partner).wait_send()

            @pl.when(i + t == 0)
            def _():
                some = pl.ds(0, ny - 1)
                rcopy(
                    S.at[r, 0, some], X.at[r, 0, some], a2a_send.at[r, i], a2a_recv.at[r, i], partner
                ).wait_send()

            return carry

        lax.fori_loop(0, half, drain, 0)


def body(side, out_grad, routing, route_probs, w_down, saved_gate, saved_up):
    nz = ny = side
    tokens, wide = out_grad.shape
    _, dc, fh = w_down.shape
    slots = saved_gate.shape[0]
    cap = slots // (nz * ny)
    top = routing.shape[1]
    half = nz // 2
    dma = pltpu.SemaphoreType.DMA
    scratch = [
        pltpu.VMEM((slots, fh), BF16),
        pltpu.VMEM((slots, fh), BF16),
        pltpu.VMEM((dc, fh), BF16),
        pltpu.VMEM((slots, fh), F32),
        pltpu.VMEM((slots, fh), F32),
        pltpu.VMEM((4, tokens, dc), BF16),
        pltpu.VMEM((4, top, tokens), jnp.int32),
        pltpu.VMEM((4, top, tokens), F32),
        pltpu.VMEM((4, nz * ny, tokens), F32),
        pltpu.VMEM((4, nz * ny, tokens), F32),
        pltpu.VMEM((4, half, ny, cap, dc), BF16),
        pltpu.VMEM((4, nz, ny, cap, dc), BF16),
        pltpu.VMEM((4, slots, fh), BF16),
        pltpu.VMEM((slots, fh), F32),
        pltpu.VMEM((dc, fh), F32),
        pltpu.VMEM((slots, fh), BF16),
        pltpu.VMEM((2, slots // 2, fh), BF16),
        pltpu.VMEM((2, slots, fh), BF16),
        pltpu.VMEM((2, slots, fh), BF16),
        pltpu.VMEM((8, 128), F32),
        pltpu.VMEM((8, 128), F32),
        dma((5,)),
        dma((4,)), dma((4,)), dma((4,)), dma((4,)),
        dma((2,)), dma((4,)), dma((4,)),
        dma((2,)), dma((2,)), dma((2,)), dma((2,)),
        dma((4, half)), dma((4, half)), dma((4, half)), dma((4, half)),
        dma((2,)), dma((2,)), dma((2, 2)), dma((2, 2)), dma((1,)), dma((1,)),
    ]
    vmem = pl.BlockSpec(memory_space=pltpu.VMEM)
    anywhere = pl.BlockSpec(memory_space=pl.ANY)
    wg, gg, gu, amax = pl.pallas_call(
        functools.partial(kernel, nz, ny),
        out_shape=(
            pltpu.VMEM((dc, fh), BF16),
            pltpu.VMEM((slots, fh), BF16),
            pltpu.VMEM((slots, fh), BF16),
            pltpu.VMEM((8, 128), F32),
        ),
        in_specs=[anywhere] * 6,
        out_specs=(vmem,) * 4,
        scratch_shapes=scratch,
        compiler_params=pltpu.CompilerParams(
            collective_id=0, has_side_effects=True, vmem_limit_bytes=65_000_000
        ),
    )(out_grad, routing.T, route_probs.T, w_down[0], saved_gate, saved_up)
    return wg.reshape(w_down.shape), gg, gu, amax[0:1, 0:1]


def solution(mesh):
    placed = (
        P(("dp", "expert"), "tensor"),
        P(("dp", "expert"), None),
        P(("dp", "expert"), None),
        P("expert", "dp", "tensor"),
        P(("dp", "expert"), "tensor"),
        P(("dp", "expert"), "tensor"),
    )
    return jax.shard_map(
        functools.partial(body, math.isqrt(mesh.shape["expert"])),
        mesh=mesh,
        in_specs=placed,
        out_specs=(
            P("expert", "dp", "tensor"),
            P(("dp", "expert"), "tensor"),
            P(("dp", "expert"), "tensor"),
            P("dp", "expert"),
        ),
        check_vma=False,
    )
```

time: 113 us -> 96.5 us (0.85)
  Pallas kernels: 107 us -> 92.7 us
  local copies, waits for them, and re-layouts: 5.43 us -> 3.02 us
    pallas_call x1, Pallas kernels: 107 us -> 92.7 us  [body(): pl.pallas_call(functools.partial(kernel, nz, ny), out_shape=(pltpu.VMEM((...]
    unnamed x7 -> x3, local copies, waits for them, and re-layouts: 4.24 us -> 2.51 us
where the time goes in v2:
time: 96.5 us; the launch traced here: 96.4 us
  Pallas kernels  92.7 us (96%)
  local copies, waits for them, and re-layouts  3.02 us (3%)
    pallas_call x1, Pallas kernels, body(): pl.pallas_call(functools.partial(kernel, nz, ny), out_shape=(pltpu.VMEM((...  92.7 us
    unnamed x3, local copies, waits for them, and re-layouts  2.51 us

profile of v2, /device:TPU:1, one launch (start us, length us, event | category | flops | bytes accessed | tf_op | source)
XLA Modules:
  0.0 96.4 jit_solution(7699000800637905786)
XLA Ops:
  0.6 92.7 %shard_map.93 = (bf16[896,512]{1,0:T(8,128)(2,1)S(1)}, bf16[512,512]{1,0:T(8,128)(2,1)S(1)}, bf16[512,512]{1,0:T(8,128)(2,1)S(1)}, f32[8,128]{1,0:T(8,128)S(1)}) custom-call(bf16[128,1792]{1,0:T(8,128)(2,1)} %og.1, s32[8,128]{1,0:T(8,128)} %bitcast.6, f32[8,128]{1,0:T(8,128)} %bitcast.7, bf16[896,512]{1,0:T(8,128)(2,1)} %bitcast.5, bf16[512,512]{1,0:T(8,128)(2,1)} %gate.1, ...), custom_call_target="tpu_custom_call" | custom-call | tf_op jit(solution)/shard_map/pallas_call | solution.py:413
  93.3 0.5 slice.3
  93.9 0.9 copy.13
  94.8 0.8 copy.14
  95.6 0.8 copy.15
